TPU v7x, 128 devices: a whole 4x4x4 slice. The times are simulated.
128 devices in a mesh: fit: 16 (over z, x), basis: 4 (over y_hi, core), occ: 2 (over y_lo).
Axes of the slice: x: 4, y: 4 (y_hi: 2, y_lo: 2; y = y_hi * 2 + y_lo), z: 4, core: 2. Of those that a mesh axis runs over, the one named last changes fastest.
Arguments:
- ints: bfloat16 [256, 12288, 128], P('fit', 'basis'), may hold values from -0.5 to 0.5
- coeffs: bfloat16 [12288, 128], P('fit', 'occ'), may hold values from -0.59765625 to 0.59765625
- offsets: int32 [192, 2], P('basis'), may hold values from 0 to 191
- mask: int32 [192, 2], P('basis'), may hold values 0 or 1
Outputs:
- exchange: float32 [12288, 4, 512], P(('fit', 'occ'), None, 'basis')
All inputs are finite; a program needn't handle non-finite values. No bound on the sum of `mask` on one device may be relied on, other than what follows from the above.
Results may differ from a plain program's by a relative error of at most 0.003.
Values may be sent and summed in bfloat16 or wider, within the bound.
A program may use at most 192 MiB of HBM per device.

v0:
```python
import jax
import jax.numpy as jnp
import numpy as np
from jax import lax
from jax.sharding import PartitionSpec as P

BLK = 64
NNZ = 2
MU_DEV = 128
SIGN_ENTRIES = (
    (0, 0, 0, 1),
    (0, 1, 1, 1),
    (0, 2, 2, 1),
    (0, 3, 3, 1),
    (1, 0, 1, -1),
    (1, 1, 0, 1),
    (1, 2, 3, -1),
    (1, 3, 2, 1),
    (2, 0, 2, -1),
    (2, 1, 3, 1),
    (2, 2, 0, 1),
    (2, 3, 1, -1),
    (3, 0, 3, -1),
    (3, 1, 2, -1),
    (3, 2, 1, 1),
    (3, 3, 0, 1),
)


def joined_along(parts, dim):
    parts = jnp.moveaxis(parts, 0, dim)
    shape = parts.shape
    return parts.reshape(*shape[:dim], shape[dim] * shape[dim + 1], *shape[dim + 2 :])


def from_everyone(shard, axis):
    size = lax.axis_size(axis)
    return lax.all_to_all(
        jnp.broadcast_to(shard[None], (size, *shard.shape)), axis, 0, 0, tiled=True
    )


def collect(shard, axis, dim):
    return joined_along(from_everyone(shard, axis), dim)


def split_up(shard, dim, size):
    shape = shard.shape
    parts = shard.reshape(*shape[:dim], size, shape[dim] // size, *shape[dim + 1 :])
    return jnp.moveaxis(parts, dim, 0)


def sum_at_owner(shard, axis, dim):
    parts = split_up(shard, dim, lax.axis_size(axis))
    arrived = lax.all_to_all(parts, axis, split_axis=0, concat_axis=0, tiled=True)
    return arrived.sum(axis=0)


def sign_table():
    table = np.zeros((4, 4, 4), np.float32)
    for entry in SIGN_ENTRIES:
        table[entry[0], entry[1], entry[2]] = entry[3]
    return table


def contract(rows_part, mixed):
    return lax.dot_general(
        rows_part, mixed, (((1,), (1,)), ((), ())), preferred_element_type=jnp.float32
    )


def shards(ints, coeffs, offsets, mask):
    full = collect(coeffs, "fit", 0)
    width = full.shape[1]
    blocks = full.reshape(-1, BLK, width)
    picked = jnp.take(blocks, offsets, axis=0) * mask[:, :, None, None].astype(jnp.bfloat16)
    picked = picked.reshape(offsets.shape[0], NNZ * BLK, width)
    aux_count, rows, stored = ints.shape
    grouped = ints.reshape(aux_count, rows // BLK, BLK, stored)
    half = jnp.einsum("arjk,rkw->rjaw", grouped, picked, preferred_element_type=jnp.float32)
    half = half.reshape(rows, aux_count * width).astype(jnp.bfloat16)
    window = half[:MU_DEV].astype(jnp.float32).reshape(MU_DEV, -1, 4)
    mixed = jnp.einsum("rqs,mkq->rmks", jnp.asarray(sign_table(), jnp.float32), window)
    mixed = mixed.reshape(4 * MU_DEV, -1).astype(jnp.bfloat16)
    terms = contract(lax.all_gather(half, "basis", axis=0, tiled=True), mixed)
    partial_fit = lax.psum_scatter(terms, "fit", scatter_dimension=0, tiled=True)
    result = sum_at_owner(partial_fit, "occ", 0)
    return result.reshape(result.shape[0], 4, MU_DEV)


def solution(mesh):
    return jax.shard_map(
        shards,
        mesh=mesh,
        in_specs=(P("fit", "basis", None), P("fit", "occ"), P("basis", None), P("basis", None)),
        out_specs=P(("fit", "occ"), None, "basis"),
        check_vma=False,
    )
```

profile of v0, /device:TPU:0, one launch (start us, length us, event | category | flops | bytes accessed | tf_op | source)
XLA Modules:
  0.0 463.8 jit_solution(10026369443056584956)
XLA Ops:
  6.5 2.2 broadcast_in_dim.26
  8.7 8.0 %all-to-all-start = ((bf16[16,768,64]{1,2,0:T(8,128)(2,1)}), bf16[16,768,64]{1,2,0:T(8,128)(2,1)}, u32[]{:S(2)}, u32[]{:S(2)}) async-start(bf16[16,768,64]{1,2,0:T(8,128)(2,1)} %broadcast_in_dim.26), calls=%async_computation | async-start | bytes 3145728 | tf_op jit(solution)/shard_map/all_to_all | solution.py:38
  16.8 0.7 convert_element_type.23
  17.8 0.7 compare_and_fusion
  18.6 0.7 compare_select_fusion
  19.5 21.8 %all-to-all-done = bf16[16,768,64]{1,2,0:T(8,128)(2,1)} async-done(((bf16[16,768,64]{1,2,0:T(8,128)(2,1)}), bf16[16,768,64]{1,2,0:T(8,128)(2,1)}, u32[]{:S(2)}, u32[]{:S(2)}) %all-to-all-start) | async-done | bytes 1572896 | tf_op jit(solution)/shard_map/all_to_all | solution.py:38
  41.4 3.1 copy.33
  44.4 2.0 gather_fusion
  46.4 1.8 copy.45
  48.3 17.7 %convert_bitcast_fusion = bf16[48,64,16,64]{1,3,2,0:T(8,128)(2,1)} fusion(bf16[16,48,64,128]{3,2,1,0:T(8,128)(2,1)} %bitcast.27, bf16[48,128,64,1]{1,0,2,3:T(8,128)(2,1)S(1)} %multiply_bitcast_fusion), kind=kOutput, calls=%fused_computation.3 | convolution fusion | flops 808452096 | bytes 19660800 | tf_op jit(solution)/shard_map/arjk,rkw->rjaw/dot_general | solution.py:80
  66.0 17.5 %copy.39 = bf16[48,64,16,64]{3,2,1,0:T(8,128)(2,1)} copy(bf16[48,64,16,64]{1,3,2,0:T(8,128)(2,1)} %convert_bitcast_fusion) | data formatting | bytes 12582912 | tf_op jit(solution)/shard_map/convert_element_type | solution.py:81
  83.6 17.3 %convert_element_type.26 = bf16[3072,1024]{1,0:T(8,128)(2,1)} reshape(bf16[48,64,16,64]{3,2,1,0:T(8,128)(2,1)} %copy.39) | data formatting | bytes 12582912 | tf_op jit(solution)/shard_map/convert_element_type | solution.py:81
  100.9 0.2 reduce-scatter.2.cloned.1.call-start
  101.1 0.5 copy.40
  101.7 0.2 reshape.31
  101.9 0.2 copy.44
  102.2 0.7 fusion.4
  102.8 1.8 copy.42
  104.7 152.5 %all-gather.2.cloned.1.call-done = bf16[12288,1024]{1,0:T(8,128)(2,1)} async-done(((bf16[3072,1024]{1,0:T(8,128)(2,1)}), bf16[12288,1024]{1,0:T(8,128)(2,1)}) %all-gather.2.cloned.1.call-update) | async-done | bytes 25165840 | tf_op jit(solution)/shard_map/all_gather | solution.py:85
  257.2 22.5 %fusion.5 = f32[12288,512]{1,0:T(8,128)} fusion(bf16[12288,1024]{1,0:T(8,128)(2,1)} %all-gather.2.cloned.1.call-done, bf16[128,8,4,128]{3,2,1,0:T(4,128)(2,1)S(1)} %bitcast.32), kind=kOutput, calls=%fused_computation.6 | convolution fusion | flops 12884901888 | bytes 51380224 | tf_op jit(solution)/shard_map/dot_general | solution.py:67
  279.7 152.8 %reduce-scatter.2.cloned.1.call-done = f32[768,512]{1,0:T(8,128)} async-done(((f32[12288,512]{1,0:T(8,128)}), f32[768,512]{1,0:T(8,128)}) %reduce-scatter.2.cloned.1.call-update) | async-done | bytes 1572880 | tf_op jit(solution)/shard_map/reduce_scatter | solution.py:86
  432.5 23.1 %all_to_all.10 = f32[2,384,512]{2,1,0:T(8,128)S(1)} all-to-all(f32[2,384,512]{2,1,0:T(8,128)} %bitcast.30), channel_id=1, replica_groups=mesh['fit'=16,'basis'=4,'occ'=2] {'occ'}, dimensions={0} | all-to-all | bytes 3145728 | tf_op jit(solution)/shard_map/all_to_all | solution.py:55
  455.6 0.2 reduce_sum.9
  455.8 1.1 reshape.33
  (16 shorter events, 0.8 us)
Async XLA Ops:
  8.7 32.6 %all-to-all-start = ((bf16[16,768,64]{1,2,0:T(8,128)(2,1)}), bf16[16,768,64]{1,2,0:T(8,128)(2,1)}, u32[]{:S(2)}, u32[]{:S(2)}) async-start(bf16[16,768,64]{1,2,0:T(8,128)(2,1)} %broadcast_in_dim.26), calls=%async_computation | async-start | bytes 3145728 | tf_op jit(solution)/shard_map/all_to_all | solution.py:38
  16.8 240.4 %all-gather.2.cloned.1.call-start = ((), (), s32[]{:S(2)}) async-start(), calls=%async_computation.3 | async-start | bytes 31457280 | tf_op jit(solution)/shard_map/all_gather | solution.py:85
  83.6 17.5 %slice-start = ((bf16[48,64,16,64]{1,3,2,0:T(8,128)(2,1)}), bf16[2,64,16,64]{1,3,2,0:T(8,128)(2,1)S(1)}, s32[]{:S(2)}) async-start(bf16[48,64,16,64]{1,3,2,0:T(8,128)(2,1)} %convert_bitcast_fusion), calls=%async_computation.5 | async-start | bytes 1048576 | tf_op jit(solution)/shard_map/slice | solution.py:82
  83.6 18.6 %copy-start = (bf16[4,4,4,1]{1,2,0,3:T(4,128)(2,1)S(1)}, bf16[4,4,4,1]{1,2,0,3:T(4,128)(2,1)}, u32[]{:S(2)}) copy-start(bf16[4,4,4,1]{1,2,0,3:T(4,128)(2,1)} %constant.32) | copy-start | bytes 388
  100.9 331.6 %reduce-scatter.2.cloned.1.call-start = ((), (), s32[]{:S(2)}) async-start(), calls=%async_computation.4 | async-start | bytes 26738688 | tf_op jit(solution)/shard_map/reduce_scatter | solution.py:86
Sparse Core Ops, SparseCore 0:
  101.0 156.1 all-gather.1
  279.8 152.6 reduce-scatter.1
where the time goes:
time: 465 us; the launch traced here: 464 us
  waiting for transfers between devices  327 us (70%)
  local copies, waits for them, and re-layouts  48.5 us (10%)
  matrix products  40.9 us (9%)
  blocking collectives  23.1 us (5%)
  between operations  13.5 us (3%)
  starting transfers between devices  8.3 us (2%)
    reduce_scatter x1, waiting for transfers between devices, shards(): lax.psum_scatter(terms, 'fit', scatter_dimension=0, tiled=True)  153 us
    all_gather x1, waiting for transfers between devices, shards(): terms = contract(lax.all_gather(half, 'basis', axis=0, tiled=True), mixed)  153 us
    convert_element_type x2, local copies, waits for them, and re-layouts, shards(): half = half.reshape(rows, aux_count * width).astype(jnp.bfloat16)  34.8 us
    all_to_all x1, blocking collectives, sum_at_owner(): lax.all_to_all(parts, axis, split_axis=0, concat_axis=0, tiled=True)  23.1 us
    dot_general x1, matrix products, contract(): lax.dot_general(rows_part, mixed, (((1,), (1,)), ((), ())), preferred_ele...  22.5 us
    all_to_all x1, waiting for transfers between devices, from_everyone(): lax.all_to_all(jnp.broadcast_to(shard[None], (size, *shard.shape)), axis,...  21.8 us
    dot_general x1, matrix products, shards(): jnp.einsum('arjk,rkw->rjaw', grouped, picked, preferred_element_type=jnp....  17.7 us
  transfers between devices with their start and end apart: 3, of which 3 were waited for; matrix products, arithmetic and copies ran while one was open for 1% of the time, Pallas kernels for 0%

commit v1 on v0

--- a/solution.py
+++ b/solution.py
@@ -82,7 +82,12 @@
     window = half[:MU_DEV].astype(jnp.float32).reshape(MU_DEV, -1, 4)
     mixed = jnp.einsum("rqs,mkq->rmks", jnp.asarray(sign_table(), jnp.float32), window)
     mixed = mixed.reshape(4 * MU_DEV, -1).astype(jnp.bfloat16)
-    terms = contract(lax.all_gather(half, "basis", axis=0, tiled=True), mixed)
+    terms = contract(
+        jnp.concatenate(
+            lax.all_to_all(jnp.stack([half] * lax.axis_size("basis")), "basis", 0, 0), axis=0
+        ),
+        mixed,
+    )
     partial_fit = lax.psum_scatter(terms, "fit", scatter_dimension=0, tiled=True)
     result = sum_at_owner(partial_fit, "occ", 0)
     return result.reshape(result.shape[0], 4, MU_DEV)

time: 465 us -> 599 us (1.29)
  waiting for transfers between devices: 327 us -> 442 us
  local copies, waits for them, and re-layouts: 48.5 us -> 59.1 us
  starting transfers between devices: 8.3 us -> 16.8 us
    all_to_all x0 -> x1, waiting for transfers between devices: none -> 271 us  [shards(): lax.all_to_all(jnp.stack([half] * lax.axis_size('basis')), 'basis', 0, 0)]
    all_gather x1 -> x0, waiting for transfers between devices: 153 us -> none  [shards(): terms = contract(lax.all_gather(half, 'basis', axis=0, tiled=True), mixed)]
    another operation x0 -> x1, local copies, waits for them, and re-layouts: none -> 10.8 us  [shards(): jnp.stack([half] * lax.axis_size('basis'))]
    all_to_all x0 -> x1, starting transfers between devices: none -> 8.55 us  [shards(): lax.all_to_all(jnp.stack([half] * lax.axis_size('basis')), 'basis', 0, 0)]
where the time goes in v1:
time: 599 us; the launch traced here: 597 us
  waiting for transfers between devices  442 us (74%)
  local copies, waits for them, and re-layouts  59.1 us (10%)
  matrix products  40.8 us (7%)
  blocking collectives  23.1 us (4%)
  starting transfers between devices  16.8 us (3%)
  between operations  13.5 us (2%)
    all_to_all x1, waiting for transfers between devices, shards(): lax.all_to_all(jnp.stack([half] * lax.axis_size('basis')), 'basis', 0, 0)  271 us
    reduce_scatter x1, waiting for transfers between devices, shards(): lax.psum_scatter(terms, 'fit', scatter_dimension=0, tiled=True)  149 us
    convert_element_type x2, local copies, waits for them, and re-layouts, shards(): half = half.reshape(rows, aux_count * width).astype(jnp.bfloat16)  34.7 us
    all_to_all x1, blocking collectives, sum_at_owner(): lax.all_to_all(parts, axis, split_axis=0, concat_axis=0, tiled=True)  23.1 us
    dot_general x1, matrix products, contract(): lax.dot_general(rows_part, mixed, (((1,), (1,)), ((), ())), preferred_ele...  22.5 us
    all_to_all x1, waiting for transfers between devices, from_everyone(): lax.all_to_all(jnp.broadcast_to(shard[None], (size, *shard.shape)), axis,...  21.9 us
    dot_general x1, matrix products, shards(): jnp.einsum('arjk,rkw->rjaw', grouped, picked, preferred_element_type=jnp....  17.6 us
  transfers between devices with their start and end apart: 3, of which 3 were waited for; matrix products, arithmetic and copies ran while one was open for 1% of the time, Pallas kernels for 0%

profile of v1, /device:TPU:0, one launch (start us, length us, event | category | flops | bytes accessed | tf_op | source)
XLA Modules:
  0.0 597.2 jit_solution(4700280571773173741)
XLA Ops:
  6.5 2.2 broadcast_in_dim.26
  8.7 8.0 %all-to-all-start = ((bf16[16,768,64]{1,2,0:T(8,128)(2,1)}), bf16[16,768,64]{1,2,0:T(8,128)(2,1)}, u32[]{:S(2)}, u32[]{:S(2)}) async-start(bf16[16,768,64]{1,2,0:T(8,128)(2,1)} %broadcast_in_dim.26), calls=%async_computation | async-start | bytes 3145728 | tf_op jit(solution)/shard_map/all_to_all | solution.py:38
  16.8 0.7 convert_element_type.25
  17.8 0.7 compare_and_fusion
  18.6 0.7 compare_select_fusion
  19.5 21.9 %all-to-all-done = bf16[16,768,64]{1,2,0:T(8,128)(2,1)} async-done(((bf16[16,768,64]{1,2,0:T(8,128)(2,1)}), bf16[16,768,64]{1,2,0:T(8,128)(2,1)}, u32[]{:S(2)}, u32[]{:S(2)}) %all-to-all-start) | async-done | bytes 1572896 | tf_op jit(solution)/shard_map/all_to_all | solution.py:38
  41.4 3.1 copy.33
  44.4 2.0 gather_fusion
  46.4 1.8 copy.45
  48.3 17.6 %convert_bitcast_fusion = bf16[48,64,16,64]{1,3,2,0:T(8,128)(2,1)} fusion(bf16[16,48,64,128]{3,2,1,0:T(8,128)(2,1)} %bitcast.28, bf16[48,128,64,1]{1,0,2,3:T(8,128)(2,1)S(1)} %multiply_bitcast_fusion), kind=kOutput, calls=%fused_computation.3 | convolution fusion | flops 808452096 | bytes 19660800 | tf_op jit(solution)/shard_map/arjk,rkw->rjaw/dot_general | solution.py:80
  65.9 17.5 %copy.39 = bf16[48,64,16,64]{3,2,1,0:T(8,128)(2,1)} copy(bf16[48,64,16,64]{1,3,2,0:T(8,128)(2,1)} %convert_bitcast_fusion) | data formatting | bytes 12582912 | tf_op jit(solution)/shard_map/convert_element_type | solution.py:81
  83.4 17.2 %convert_element_type.28 = bf16[3072,1024]{1,0:T(8,128)(2,1)} reshape(bf16[48,64,16,64]{3,2,1,0:T(8,128)(2,1)} %copy.39) | data formatting | bytes 12582912 | tf_op jit(solution)/shard_map/convert_element_type | solution.py:81
  100.7 10.8 %stack.2 = bf16[4,3072,1024]{2,1,0:T(8,128)(2,1)} broadcast(bf16[3072,1024]{1,0:T(8,128)(2,1)} %convert_element_type.28), dimensions={1,2} | broadcast | bytes 31457280 | tf_op jit(solution)/shard_map/stack | solution.py:87
  111.4 8.5 %all-to-all-start.1 = ((bf16[4,3072,1024]{2,1,0:T(8,128)(2,1)}), bf16[4,3072,1024]{2,1,0:T(8,128)(2,1)}, u32[]{:S(2)}, u32[]{:S(2)}) async-start(bf16[4,3072,1024]{2,1,0:T(8,128)(2,1)} %stack.2), calls=%async_computation.1 | async-start | bytes 50331648 | tf_op jit(solution)/shard_map/all_to_all | solution.py:87
  120.2 0.5 copy.40
  120.8 0.2 reshape.38
  121.0 0.2 copy.44
  121.2 0.7 fusion.4
  121.9 1.8 copy.42
  123.8 270.6 %all-to-all-done.1 = bf16[4,3072,1024]{2,1,0:T(8,128)(2,1)} async-done(((bf16[4,3072,1024]{2,1,0:T(8,128)(2,1)}), bf16[4,3072,1024]{2,1,0:T(8,128)(2,1)}, u32[]{:S(2)}, u32[]{:S(2)}) %all-to-all-start.1) | async-done | bytes 25165856 | tf_op jit(solution)/shard_map/all_to_all | solution.py:87
  394.4 22.5 %fusion.5 = f32[12288,512]{1,0:T(8,128)} fusion(bf16[12288,1024]{1,0:T(8,128)(2,1)} %bitcast.6, bf16[128,8,4,128]{3,2,1,0:T(4,128)(2,1)S(1)} %bitcast.33), kind=kOutput, calls=%fused_computation.6 | convolution fusion | flops 12884901888 | bytes 51380224 | tf_op jit(solution)/shard_map/dot_general | solution.py:67
  416.9 149.1 %reduce-scatter.2.cloned.1.call-done = f32[768,512]{1,0:T(8,128)} async-done(((f32[12288,512]{1,0:T(8,128)}), f32[768,512]{1,0:T(8,128)}) %reduce-scatter.2.cloned.1.call-update) | async-done | bytes 1572880 | tf_op jit(solution)/shard_map/reduce_scatter | solution.py:91
  566.0 23.1 %all_to_all.15 = f32[2,384,512]{2,1,0:T(8,128)S(1)} all-to-all(f32[2,384,512]{2,1,0:T(8,128)} %bitcast.31), channel_id=1, replica_groups=mesh['fit'=16,'basis'=4,'occ'=2] {'occ'}, dimensions={0} | all-to-all | bytes 3145728 | tf_op jit(solution)/shard_map/all_to_all | solution.py:55
  589.2 1.1 reshape.40
  (16 shorter events, 1.1 us)
Async XLA Ops:
  8.7 32.6 %all-to-all-start = ((bf16[16,768,64]{1,2,0:T(8,128)(2,1)}), bf16[16,768,64]{1,2,0:T(8,128)(2,1)}, u32[]{:S(2)}, u32[]{:S(2)}) async-start(bf16[16,768,64]{1,2,0:T(8,128)(2,1)} %broadcast_in_dim.26), calls=%async_computation | async-start | bytes 3145728 | tf_op jit(solution)/shard_map/all_to_all | solution.py:38
  111.4 8.8 %slice-start = ((bf16[48,64,16,64]{1,3,2,0:T(8,128)(2,1)}), bf16[2,64,16,64]{1,3,2,0:T(8,128)(2,1)S(1)}, s32[]{:S(2)}) async-start(bf16[48,64,16,64]{1,3,2,0:T(8,128)(2,1)} %convert_bitcast_fusion), calls=%async_computation.5 | async-start | bytes 1048576 | tf_op jit(solution)/shard_map/slice | solution.py:82
  111.4 9.8 %copy-start = (bf16[4,4,4,1]{1,2,0,3:T(4,128)(2,1)S(1)}, bf16[4,4,4,1]{1,2,0,3:T(4,128)(2,1)}, u32[]{:S(2)}) copy-start(bf16[4,4,4,1]{1,2,0,3:T(4,128)(2,1)} %constant.32) | copy-start | bytes 388
  111.4 283.0 %all-to-all-start.1 = ((bf16[4,3072,1024]{2,1,0:T(8,128)(2,1)}), bf16[4,3072,1024]{2,1,0:T(8,128)(2,1)}, u32[]{:S(2)}, u32[]{:S(2)}) async-start(bf16[4,3072,1024]{2,1,0:T(8,128)(2,1)} %stack.2), calls=%async_computation.1 | async-start | bytes 50331648 | tf_op jit(solution)/shard_map/all_to_all | solution.py:87
  120.0 446.0 %reduce-scatter.2.cloned.1.call-start = ((), (), s32[]{:S(2)}) async-start(), calls=%async_computation.4 | async-start | bytes 26738688 | tf_op jit(solution)/shard_map/reduce_scatter | solution.py:91
Sparse Core Ops, SparseCore 0:
  417.0 148.9 reduce-scatter.1
